TPU v7x, 32 devices: a whole 2x2x4 slice. The times are simulated.
32 devices in a mesh: seqa: 4 (over x, core), seqb: 8 (over z, y).
Axes of the slice: x: 2, y: 2, z: 4, core: 2. Of those that a mesh axis runs over, the one named last changes fastest.
Arguments:
- sequence_input: bfloat16 [16384, 640], P(('seqa', 'seqb')), may hold values from -6 to 6
- w_prev: bfloat16 [3, 640, 1280], P(None, 'seqa'), may hold values from -0.15625 to 0.15625
- w_now: bfloat16 [3, 640, 1280], P(None, 'seqa'), may hold values from -0.15625 to 0.15625
- conv_bias: float32 [3, 1280], replicated, may hold values from -4 to 4
- w_mix: bfloat16 [3, 640, 640], P(None, None, 'seqa'), may hold values from -0.25 to 0.25
Outputs:
- seq_out: bfloat16 [16384, 640], P(('seqa', 'seqb'))
All inputs are finite; a program needn't handle non-finite values.
Results may differ from a plain program's by a relative error of at most 0.0052.
Values may be sent and summed in bfloat16 or wider, within the bound.
A program may use at most 64 MiB of HBM per device.

v0:
```python
import jax
import jax.numpy as jnp
from jax import lax
from jax.sharding import PartitionSpec as P

D = 640
DILATION_FIRST1 = 128
DILATION_SECOND2 = 512
DILATION_THIRD3 = 2048


def from_behind(value, axis, by):
    peers = lax.axis_size(axis)
    pairs = [(i, i + by) for i in range(peers) if 0 <= i + by < peers]
    return lax.ppermute(value, axis, pairs)


def norm_rows(values):
    scale = lax.rsqrt(jnp.mean(values * values, axis=1, keepdims=True) + 1e-06)
    return (values * scale).astype(jnp.bfloat16)


def block_prior(normed, dilation_step):
    rows = normed.shape[0]
    whole = dilation_step // rows
    part = dilation_step % rows
    pieces = []
    if part > 0:
        pieces.append(from_behind(normed[rows - part :], ("seqa", "seqb"), whole + 1))
    head = normed[: rows - part]
    if whole > 0:
        head = from_behind(head, ("seqa", "seqb"), whole)
    pieces.append(head)
    return jnp.concatenate(pieces, axis=0)


def one_layer(hidden_state, tap_prev, tap_now, bias, mixing, dilation_step):
    normed = norm_rows(hidden_state)
    earlier = block_prior(normed, dilation_step)
    rows = hidden_state.shape[0]
    start_sum = jnp.broadcast_to(bias[None, :], (rows, bias.shape[0]))
    total = start_sum
    total = total + jnp.dot(
        earlier,
        lax.all_gather(tap_prev, "seqa", axis=0, tiled=True),
        preferred_element_type=jnp.float32,
    )
    pre = total + jnp.dot(
        normed,
        lax.all_gather(tap_now, "seqa", axis=0, tiled=True),
        preferred_element_type=jnp.float32,
    )
    hidden = (pre[:, :D] * jax.nn.sigmoid(pre[:, D:])).astype(jnp.bfloat16)
    return hidden_state + jnp.dot(
        hidden,
        lax.all_gather(mixing, "seqa", axis=1, tiled=True),
        preferred_element_type=jnp.float32,
    )


def local(sequence_input, w_prev, w_now, conv_bias, w_mix):
    hidden_state = sequence_input.astype(jnp.float32)
    for layer_index, dilation_step in enumerate(
        (DILATION_FIRST1, DILATION_SECOND2, DILATION_THIRD3)
    ):
        hidden_state = one_layer(
            hidden_state,
            w_prev[layer_index],
            w_now[layer_index],
            conv_bias[layer_index],
            w_mix[layer_index],
            dilation_step,
        )
    block_output = hidden_state.astype(jnp.bfloat16)
    return block_output


def solution(mesh):
    return jax.shard_map(
        local,
        mesh=mesh,
        in_specs=(
            P(("seqa", "seqb"), None),
            P(None, "seqa", None),
            P(None, "seqa", None),
            P(),
            P(None, None, "seqa"),
        ),
        out_specs=P(("seqa", "seqb"), None),
        check_vma=False,
    )
```

profile of v0, /device:TPU:29, one launch (start us, length us, event | category | flops | bytes accessed | tf_op | source)
XLA Modules:
  0.0 172.0 jit_solution(16757699871526327815)
XLA Ops:
  6.5 2.4 %fusion.47 = (bf16[1,160,1280]{2,1,0:T(8,128)(2,1)}, bf16[1,160,1280]{2,1,0:T(8,128)(2,1)}, bf16[1,160,1280]{2,1,0:T(8,128)(2,1)}) fusion(bf16[3,160,1280]{2,1,0:T(8,128)(2,1)} %param.7), kind=kLoop, calls=%fused_computation.65 | loop fusion | bytes 2457600 | tf_op jit(solution)/shard_map/slice | solution.py:69
  9.0 0.0 all-gather.18.cloned.1.call-update
  9.0 0.0 all-gather.16.cloned.1.call-start
  9.1 1.1 fusion.46
  10.2 0.0 all-gather.16.cloned.1.call-update
  10.2 0.0 all-gather.22.cloned.1.call-start
  10.2 0.7 all-gather.22.cloned.1.call-update
  10.9 0.0 all-gather.20.cloned.1.call-start
  11.0 0.5 all-gather.20.cloned.1.call-update
  11.5 0.0 all-gather.26.cloned.1.call-start
  11.5 0.5 all-gather.26.cloned.1.call-update
  12.1 0.0 all-gather.24.cloned.1.call-start
  12.1 0.2 fusion.13
  12.4 0.0 copy-start.12
  12.4 0.0 copy-start.11
  12.4 0.2 fusion.14
  12.6 0.0 copy-start.1
  12.6 0.7 slice.80
  13.3 3.3 %collective-permute-start = (bf16[128,640]{1,0:T(8,128)(2,1)}, bf16[128,640]{1,0:T(8,128)(2,1)}, u32[]{:S(2)}, u32[]{:S(2)}) collective-permute-start(bf16[128,640]{1,0:T(8,128)(2,1)} %slice.80), channel_id=1, source_target_pairs={{0,1},{1,2},{2,3},{3,4},{4,5},{5,6},{6,7},{7,8},{8,9},{9,10},{10,1... | collective-permute-start | bytes 491528 | tf_op jit(solution)/shard_map/ppermute | solution.py:15
  16.6 0.0 all-gather.24.cloned.1.call-update
  16.6 0.9 slice.81
  17.5 0.7 fusion.48
  18.2 13.4 %all-gather.2 = bf16[1,640,640]{1,2,0:T(8,128)(2,1)} all-gather(bf16[1,640,160]{1,2,0:T(8,128)(2,1)S(1)} %get-tuple-element.15), channel_id=4, replica_groups=mesh['seqa'=4,'seqb'=8] {'seqa'}, dimensions={2}, use_global_device_ids=true | all-gather | bytes 1024000 | tf_op jit(solution)/shard_map/all_gather | solution.py:56
  31.6 3.2 %all-gather.18.cloned.1.call-done = bf16[1,640,1280]{2,1,0:T(8,128)(2,1)} async-done(((bf16[1,160,1280]{2,1,0:T(8,128)(2,1)}), bf16[1,640,1280]{2,1,0:T(8,128)(2,1)}) %all-gather.18.cloned.1.call-update) | async-done | bytes 1638416 | tf_op jit(solution)/shard_map/all_gather | solution.py:50
  34.9 2.8 %fusion.9 = f32[512,1280]{1,0:T(8,128)S(1)} fusion(bf16[512,640]{1,0:T(8,128)(2,1)} %copy-done.1, bf16[1,640,1280]{2,1,0:T(8,128)(2,1)} %all-gather.18.cloned.1.call-done), kind=kOutput, calls=%fused_computation.15 | convolution fusion | flops 838860800 | bytes 4915200 | tf_op jit(solution)/shard_map/dot_general | solution.py:48
  37.7 0.0 collective-permute-done
  37.7 18.8 %all-gather.16.cloned.1.call-done = bf16[1,640,1280]{2,1,0:T(8,128)(2,1)} async-done(((bf16[1,160,1280]{2,1,0:T(8,128)(2,1)}), bf16[1,640,1280]{2,1,0:T(8,128)(2,1)}) %all-gather.16.cloned.1.call-update) | async-done | bytes 1638416 | tf_op jit(solution)/shard_map/all_gather | solution.py:45
  56.5 2.9 %fusion = f32[512,1280]{1,0:T(8,128)S(1)} fusion(f32[512,1280]{1,0:T(8,128)S(1)} %fusion.9, bf16[1,640,1280]{2,1,0:T(8,128)(2,1)} %all-gather.16.cloned.1.call-done, f32[1280]{0:T(1024)S(1)} %get-tuple-element.6, bf16[384,640]{1,0:T(8,128)(2,1)} %slice.81, bf16[128,640]{1,0:T(8,128)(2,1)} %collective-permute-done), kind=kOutput, calls=%fused_computation.3 | convolution fusion | flops 841482240 | bytes 7541760 | tf_op jit(solution)/shard_map/dot_general | solution.py:43
  59.4 1.0 multiply_reduce_fusion.1
  60.4 1.0 copy-done.4
  61.5 1.0 multiply_convert_fusion.1
  62.4 2.1 %collective-permute-start.1 = (bf16[512,640]{1,0:T(8,128)(2,1)}, bf16[512,640]{1,0:T(8,128)(2,1)}, u32[]{:S(2)}, u32[]{:S(2)}) collective-permute-start(bf16[512,640]{1,0:T(8,128)(2,1)} %multiply_convert_fusion.1), channel_id=1, source_target_pairs={{0,1},{1,2},{2,3},{3,4},{4,5},{5,6},{6,7},{7,8},{8,9},{9,10},{10,1... | collective-permute-start | bytes 1966088 | tf_op jit(solution)/shard_map/ppermute | solution.py:15
  64.5 14.2 %all-gather.5 = bf16[1,640,640]{1,2,0:T(8,128)(2,1)} all-gather(bf16[1,640,160]{1,2,0:T(8,128)(2,1)S(1)} %copy-done.7), channel_id=7, replica_groups=mesh['seqa'=4,'seqb'=8] {'seqa'}, dimensions={2}, use_global_device_ids=true | all-gather | bytes 1024000 | tf_op jit(solution)/shard_map/all_gather | solution.py:56
  78.7 3.8 %all-gather.22.cloned.1.call-done = bf16[1,640,1280]{2,1,0:T(8,128)(2,1)} async-done(((bf16[1,160,1280]{2,1,0:T(8,128)(2,1)}), bf16[1,640,1280]{2,1,0:T(8,128)(2,1)}) %all-gather.22.cloned.1.call-update) | async-done | bytes 1638416 | tf_op jit(solution)/shard_map/all_gather | solution.py:50
  82.5 2.8 %fusion.6 = f32[512,1280]{1,0:T(8,128)S(1)} fusion(bf16[512,640]{1,0:T(8,128)(2,1)} %multiply_convert_fusion.1, bf16[1,640,1280]{2,1,0:T(8,128)(2,1)} %all-gather.22.cloned.1.call-done), kind=kOutput, calls=%fused_computation.12 | convolution fusion | flops 838860800 | bytes 4915200 | tf_op jit(solution)/shard_map/dot_general | solution.py:48
  85.3 22.9 %all-gather.20.cloned.1.call-done = bf16[1,640,1280]{2,1,0:T(8,128)(2,1)} async-done(((bf16[1,160,1280]{2,1,0:T(8,128)(2,1)}), bf16[1,640,1280]{2,1,0:T(8,128)(2,1)}) %all-gather.20.cloned.1.call-update) | async-done | bytes 1638416 | tf_op jit(solution)/shard_map/all_gather | solution.py:45
  108.1 0.0 collective-permute-done.1
  108.2 3.0 %fusion.1 = f32[512,1280]{1,0:T(8,128)S(1)} fusion(f32[512,1280]{1,0:T(8,128)S(1)} %fusion.6, bf16[512,640]{1,0:T(8,128)(2,1)} %collective-permute-done.1, bf16[1,640,1280]{2,1,0:T(8,128)(2,1)} %all-gather.20.cloned.1.call-done, f32[1280]{0:T(1024)S(1)} %get-tuple-element.7), kind=kOutput, calls=%fused_computation.4 | convolution fusion | flops 840171520 | bytes 7541760 | tf_op jit(solution)/shard_map/dot_general | solution.py:43
  111.2 1.0 multiply_reduce_fusion
  112.2 1.1 copy-done.2
  113.2 1.0 multiply_convert_fusion
  114.2 2.3 %collective-permute-start.2 = (bf16[512,640]{1,0:T(8,128)(2,1)}, bf16[512,640]{1,0:T(8,128)(2,1)S(1)}, u32[]{:S(2)}, u32[]{:S(2)}) collective-permute-start(bf16[512,640]{1,0:T(8,128)(2,1)} %multiply_convert_fusion), channel_id=1, source_target_pairs={{0,4},{1,5},{2,6},{3,7},{4,8},{5,9},{6,10},{7,11},{8,12},{9,13},{1... | collective-permute-start | bytes 1966088 | tf_op jit(solution)/shard_map/ppermute | solution.py:15
  116.5 14.1 %all-gather.8 = bf16[1,640,640]{1,2,0:T(8,128)(2,1)} all-gather(bf16[1,640,160]{1,2,0:T(8,128)(2,1)S(1)} %get-tuple-element.14), channel_id=10, replica_groups=mesh['seqa'=4,'seqb'=8] {'seqa'}, dimensions={2}, use_global_device_ids=true | all-gather | bytes 1024000 | tf_op jit(solution)/shard_map/all_gather | solution.py:56
  130.6 3.4 %all-gather.26.cloned.1.call-done = bf16[1,640,1280]{2,1,0:T(8,128)(2,1)} async-done(((bf16[1,160,1280]{2,1,0:T(8,128)(2,1)}), bf16[1,640,1280]{2,1,0:T(8,128)(2,1)}) %all-gather.26.cloned.1.call-update) | async-done | bytes 1638416 | tf_op jit(solution)/shard_map/all_gather | solution.py:50
  134.0 2.8 %fusion.3 = f32[512,1280]{1,0:T(8,128)S(1)} fusion(bf16[512,640]{1,0:T(8,128)(2,1)} %multiply_convert_fusion, bf16[1,640,1280]{2,1,0:T(8,128)(2,1)} %all-gather.26.cloned.1.call-done), kind=kOutput, calls=%fused_computation.9 | convolution fusion | flops 838860800 | bytes 4915200 | tf_op jit(solution)/shard_map/dot_general | solution.py:48
  136.8 23.8 %all-gather.24.cloned.1.call-done = bf16[1,640,1280]{2,1,0:T(8,128)(2,1)} async-done(((bf16[1,160,1280]{2,1,0:T(8,128)(2,1)}), bf16[1,640,1280]{2,1,0:T(8,128)(2,1)}) %all-gather.24.cloned.1.call-update) | async-done | bytes 1638416 | tf_op jit(solution)/shard_map/all_gather | solution.py:45
  160.6 2.8 %fusion.2 = f32[512,1280]{1,0:T(8,128)S(1)} fusion(f32[512,1280]{1,0:T(8,128)S(1)} %fusion.3, bf16[512,640]{1,0:T(8,128)(2,1)S(1)} %collective-permute-done.2, bf16[1,640,1280]{2,1,0:T(8,128)(2,1)} %all-gather.24.cloned.1.call-done, f32[1280]{0:T(1024)S(1)} %get-tuple-element.5), kind=kOutput, calls=%fused_computation.5 | convolution fusion | flops 840171520 | bytes 7541760 | tf_op jit(solution)/shard_map/dot_general | solution.py:43
  163.4 1.7 %fusion.12 = bf16[512,640]{1,0:T(8,128)(2,1)} fusion(f32[512,640]{1,0:T(8,128)S(1)} %copy-done.3, bf16[1,640,640]{1,2,0:T(8,128)(2,1)S(1)} %copy-done.10, f32[512,1280]{1,0:T(8,128)S(1)} %fusion.2), kind=kOutput, calls=%fused_computation.20 | convolution fusion | flops 421724160 | bytes 5406720 | tf_op jit(solution)/shard_map/dot_general | solution.py:54
  (27 shorter events, 0.1 us)
Async XLA Ops:
  6.5 2.5 %copy-start.6 = (bf16[3,160,1280]{2,1,0:T(8,128)(2,1)S(1)}, bf16[3,160,1280]{2,1,0:T(8,128)(2,1)}, u32[]{:S(2)}) copy-start(bf16[3,160,1280]{2,1,0:T(8,128)(2,1)} %param.6) | copy-start | bytes 3686404
  6.5 28.3 %all-gather.18.cloned.1.call-start = ((), (), s32[]{:S(2)}) async-start(), calls=%async_computation.1 | async-start | bytes 2048000 | tf_op jit(solution)/shard_map/all_gather | solution.py:50
  9.0 47.5 %all-gather.16.cloned.1.call-start = ((), (), s32[]{:S(2)}) async-start(), calls=%async_computation | async-start | bytes 2048000 | tf_op jit(solution)/shard_map/all_gather | solution.py:45
  10.2 2.0 %copy-start = (bf16[512,640]{1,0:T(8,128)(2,1)S(1)}, bf16[512,640]{1,0:T(8,128)(2,1)}, u32[]{:S(2)}) copy-start(bf16[512,640]{1,0:T(8,128)(2,1)} %param.5) | copy-start | bytes 1966084
  10.2 72.3 %all-gather.22.cloned.1.call-start = ((), (), s32[]{:S(2)}) async-start(), calls=%async_computation.3 | async-start | bytes 2048000 | tf_op jit(solution)/shard_map/all_gather | solution.py:50
  10.9 97.2 %all-gather.20.cloned.1.call-start = ((), (), s32[]{:S(2)}) async-start(), calls=%async_computation.2 | async-start | bytes 2048000 | tf_op jit(solution)/shard_map/all_gather | solution.py:45
  11.5 122.5 %all-gather.26.cloned.1.call-start = ((), (), s32[]{:S(2)}) async-start(), calls=%async_computation.5 | async-start | bytes 2048000 | tf_op jit(solution)/shard_map/all_gather | solution.py:50
  12.1 148.5 %all-gather.24.cloned.1.call-start = ((), (), s32[]{:S(2)}) async-start(), calls=%async_computation.4 | async-start | bytes 2048000 | tf_op jit(solution)/shard_map/all_gather | solution.py:45
  12.4 5.1 %copy-start.12 = (f32[3,1280]{1,0:T(4,128)S(1)}, f32[3,1280]{1,0:T(4,128)}, u32[]{:S(2)}) copy-start(f32[3,1280]{1,0:T(4,128)} %param.8) | copy-start | bytes 46084
  12.4 5.1 %copy-start.11 = (bf16[3,640,160]{1,2,0:T(8,128)(2,1)S(1)}, bf16[3,640,160]{1,2,0:T(8,128)(2,1)}, u32[]{:S(2)}) copy-start(bf16[3,640,160]{1,2,0:T(8,128)(2,1)} %param.9) | copy-start | bytes 1843204
  12.6 5.7 %copy-start.1 = (bf16[512,640]{1,0:T(8,128)(2,1)}, bf16[512,640]{1,0:T(8,128)(2,1)S(1)}, u32[]{:S(2)}) copy-start(bf16[512,640]{1,0:T(8,128)(2,1)S(1)} %fusion.14) | copy-start | bytes 1966084
  13.3 24.4 %collective-permute-start = (bf16[128,640]{1,0:T(8,128)(2,1)}, bf16[128,640]{1,0:T(8,128)(2,1)}, u32[]{:S(2)}, u32[]{:S(2)}) collective-permute-start(bf16[128,640]{1,0:T(8,128)(2,1)} %slice.80), channel_id=1, source_target_pairs={{0,1},{1,2},{2,3},{3,4},{4,5},{5,6},{6,7},{7,8},{8,9},{9,10},{10,1... | collective-permute-start | bytes 491528 | tf_op jit(solution)/shard_map/ppermute | solution.py:15
  56.5 2.9 %copy-start.8 = (bf16[1,640,640]{1,2,0:T(8,128)(2,1)S(1)}, bf16[1,640,640]{1,2,0:T(8,128)(2,1)}, u32[]{:S(2)}) copy-start(bf16[1,640,640]{1,2,0:T(8,128)(2,1)} %all-gather.2) | copy-start | bytes 2457604
  60.4 1.1 copy-start.4
  60.4 4.1 %copy-start.7 = (bf16[1,640,160]{1,2,0:T(8,128)(2,1)S(1)}, bf16[1,640,160]{1,2,0:T(8,128)(2,1)}, u32[]{:S(2)}) copy-start(bf16[1,640,160]{1,2,0:T(8,128)(2,1)} %get-tuple-element.16) | copy-start | bytes 614404
  62.4 45.7 %collective-permute-start.1 = (bf16[512,640]{1,0:T(8,128)(2,1)}, bf16[512,640]{1,0:T(8,128)(2,1)}, u32[]{:S(2)}, u32[]{:S(2)}) collective-permute-start(bf16[512,640]{1,0:T(8,128)(2,1)} %multiply_convert_fusion.1), channel_id=1, source_target_pairs={{0,1},{1,2},{2,3},{3,4},{4,5},{5,6},{6,7},{7,8},{8,9},{9,10},{10,1... | collective-permute-start | bytes 1966088 | tf_op jit(solution)/shard_map/ppermute | solution.py:15
  108.2 3.0 %copy-start.5 = (f32[512,640]{1,0:T(8,128)S(1)}, f32[512,640]{1,0:T(8,128)}, u32[]{:S(2)}) copy-start(f32[512,640]{1,0:T(8,128)} %copy-done.4) | copy-start | bytes 3932164
  108.2 3.0 %copy-start.9 = (bf16[1,640,640]{1,2,0:T(8,128)(2,1)S(1)}, bf16[1,640,640]{1,2,0:T(8,128)(2,1)}, u32[]{:S(2)}) copy-start(bf16[1,640,640]{1,2,0:T(8,128)(2,1)} %all-gather.5) | copy-start | bytes 2457604
  112.1 1.1 copy-start.2
  114.2 46.4 %collective-permute-start.2 = (bf16[512,640]{1,0:T(8,128)(2,1)}, bf16[512,640]{1,0:T(8,128)(2,1)S(1)}, u32[]{:S(2)}, u32[]{:S(2)}) collective-permute-start(bf16[512,640]{1,0:T(8,128)(2,1)} %multiply_convert_fusion), channel_id=1, source_target_pairs={{0,4},{1,5},{2,6},{3,7},{4,8},{5,9},{6,10},{7,11},{8,12},{9,13},{1... | collective-permute-start | bytes 1966088 | tf_op jit(solution)/shard_map/ppermute | solution.py:15
  160.6 2.8 %copy-start.3 = (f32[512,640]{1,0:T(8,128)S(1)}, f32[512,640]{1,0:T(8,128)}, u32[]{:S(2)}) copy-start(f32[512,640]{1,0:T(8,128)} %copy-done.2) | copy-start | bytes 3932164
  160.6 2.8 %copy-start.10 = (bf16[1,640,640]{1,2,0:T(8,128)(2,1)S(1)}, bf16[1,640,640]{1,2,0:T(8,128)(2,1)}, u32[]{:S(2)}) copy-start(bf16[1,640,640]{1,2,0:T(8,128)(2,1)} %all-gather.8) | copy-start | bytes 2457604
Sparse Core Ops, SparseCore 0:
  9.1 25.6 all-gather.17
  36.4 19.9 all-gather.15
  58.0 24.3 all-gather.21
  83.9 24.2 all-gather.19
  109.6 24.3 all-gather.25
  135.4 25.1 all-gather.23
where the time goes:
time: 174 us; the launch traced here: 172 us
  waiting for transfers between devices  77.6 us (45%)
  blocking collectives  41.6 us (24%)
  matrix products  20.8 us (12%)
  between operations  13.7 us (8%)
  local copies, waits for them, and re-layouts  8.03 us (5%)
  starting transfers between devices  7.82 us (4%)
  other arithmetic  2.36 us (1%)
    all_gather x3, waiting for transfers between devices, one_layer(): lax.all_gather(tap_prev, 'seqa', axis=0, tiled=True)  65.4 us
    all_gather x3, blocking collectives, one_layer(): lax.all_gather(mixing, 'seqa', axis=1, tiled=True)  41.6 us
    all_gather x3, waiting for transfers between devices, one_layer(): lax.all_gather(tap_now, 'seqa', axis=0, tiled=True)  10.4 us
    dot_general x3, matrix products, one_layer(): jnp.dot(earlier, lax.all_gather(tap_prev, 'seqa', axis=0, tiled=True), pr...  8.68 us
    dot_general x3, matrix products, one_layer(): jnp.dot(normed, lax.all_gather(tap_now, 'seqa', axis=0, tiled=True), pref...  8.46 us
    ppermute x3, starting transfers between devices, from_behind(): return lax.ppermute(value, axis, pairs)  7.62 us
    dot_general x3, matrix products, one_layer(): jnp.dot(hidden, lax.all_gather(mixing, 'seqa', axis=1, tiled=True), prefe...  3.7 us
  transfers between devices with their start and end apart: 9, of which 6 were waited for; matrix products, arithmetic and copies ran while one was open for 13% of the time, Pallas kernels for 0%

commit v1 on v0

v1 whole, which is shorter than its diff:
```python
import functools

import jax
import jax.numpy as jnp
from jax import lax
from jax.experimental import pallas as pl
from jax.experimental.pallas import tpu as pltpu
from jax.sharding import PartitionSpec as P

DILATIONS = (128, 512, 2048)
EPS = 1e-06
TILE = 16
GROUP = 4
MESH_ID = pl.DeviceIdType.MESH


def from_behind(value, axis, by):
    peers = lax.axis_size(axis)
    pairs = [(i, i + by) for i in range(peers) if 0 <= i + by < peers]
    return lax.ppermute(value, axis, pairs)


def norm_rows(values):
    scale = lax.rsqrt(jnp.mean(values * values, axis=1, keepdims=True) + EPS)
    return (values * scale).astype(jnp.bfloat16)


def block_prior(normed, dilation_step):
    rows = normed.shape[0]
    whole = dilation_step // rows
    part = dilation_step % rows
    pieces = []
    if part > 0:
        pieces.append(from_behind(normed[rows - part :], ("seqa", "seqb"), whole + 1))
    head = normed[: rows - part]
    if whole > 0:
        head = from_behind(head, ("seqa", "seqb"), whole)
    pieces.append(head)
    return jnp.concatenate(pieces, axis=0)


def one_layer(hidden_state, tap_prev, tap_now, bias, mixing, dilation_step):
    normed = norm_rows(hidden_state)
    earlier = block_prior(normed, dilation_step)
    dim = hidden_state.shape[1]
    pre = bias[None, :] + jnp.dot(
        earlier,
        lax.all_gather(tap_prev, "seqa", axis=0, tiled=True),
        preferred_element_type=jnp.float32,
    )
    pre = pre + jnp.dot(
        normed,
        lax.all_gather(tap_now, "seqa", axis=0, tiled=True),
        preferred_element_type=jnp.float32,
    )
    hidden = (pre[:, :dim] * jax.nn.sigmoid(pre[:, dim:])).astype(jnp.bfloat16)
    return hidden_state + jnp.dot(
        hidden,
        lax.all_gather(mixing, "seqa", axis=1, tiled=True),
        preferred_element_type=jnp.float32,
    )


def plain_local(sequence_input, w_prev, w_now, conv_bias, w_mix):
    state = sequence_input.astype(jnp.float32)
    for layer, step in enumerate(DILATIONS):
        state = one_layer(
            state, w_prev[layer], w_now[layer], conv_bias[layer], w_mix[layer], step
        )
    return state.astype(jnp.bfloat16)


def flip(value, bit):
    return value + bit - 2 * bit * ((value // bit) % 2)


def block_kernel(
    na, nb, chunk,
    x_hbm, wp_hbm, wn_hbm, bias_ref, wm_hbm,
    out_ref,
    w, xin, tail, state, u0, u1, u2, h1, h2, pre,
    load_sem, x_sem, send, recv, halo_send, halo_recv,
):
    layers, dim = wp_hbm.shape[0], x_hbm.shape[1]
    wide = 2 * dim
    shard = wp_hbm.shape[1]
    rows = x_hbm.shape[0]
    n = na * nb
    part = DILATIONS[0]
    chunks = rows // chunk
    a, b = lax.axis_index("seqa"), lax.axis_index("seqb")
    me = a * nb + b
    a1, a2 = flip(a, 1), flip(a, 2)
    b1, b2 = flip(b, 1), flip(b, 2)
    p = b % GROUP
    p1, p2 = flip(p, 1), flip(p, 2)
    p3 = flip(p1, 2)
    big = 2 * TILE
    direct = GROUP * big

    def at(index):
        return (index // nb, index % nb)

    hops = (1, DILATIONS[1] // rows, DILATIONS[2] // rows)

    loads = []
    for l in range(layers):
        loads.append([
            pltpu.make_async_copy(wp_hbm.at[l], w.at[l, a, :, pl.ds(0, wide)], load_sem.at[l, 0]),
            pltpu.make_async_copy(wn_hbm.at[l], w.at[l, a, :, pl.ds(wide, wide)], load_sem.at[l, 1]),
            pltpu.make_async_copy(wm_hbm.at[l], w.at[l, a, :, pl.ds(2 * wide, dim)], load_sem.at[l, 2]),
        ])
    for c in loads[0]:
        c.start()
    x_load = pltpu.make_async_copy(x_hbm, xin, x_sem)
    x_load.start()
    for l in range(1, layers):
        for c in loads[l]:
            c.start()

    barrier = pltpu.get_barrier_semaphore()
    near = [(a1, b), (a2, b), (a, b1), (a, b2)]
    for h in sorted(set(hops)):
        near += [at((me + h) % n), at((me + n - h) % n)]
    for dev in near:
        pl.semaphore_signal(barrier, inc=1, device_id=dev, device_id_type=MESH_ID)
    pl.semaphore_wait(barrier, len(near))

    def move(l, k, owner, start, size, dev):
        ref = w.at[l, owner, pl.ds(pl.multiple_of(start, TILE), size)]
        return pltpu.make_async_remote_copy(
            src_ref=ref, dst_ref=ref, send_sem=send.at[l, k], recv_sem=recv.at[l, k],
            device_id=dev, device_id_type=MESH_ID,
        )

    core, across, ynear, znear = (a1, b), (a2, b), (a, b1), (a, b2)
    moves = []
    for l in range(layers):
        moves.append([
            move(l, 0, a, p * big, big, across),
            move(l, 1, a, direct, shard - direct, across),
            move(l, 2, a, 0, shard, core),
            move(l, 3, a2, p * big, big, ynear),
            move(l, 4, a2, p * big, big, znear),
            move(l, 5, a2, p * big, big, core),
            move(l, 6, a2, direct, shard - direct, core),
            move(l, 7, a2, p1 * big, TILE, znear),
            move(l, 8, a2, p1 * big, big, core),
            move(l, 9, a2, p2 * big + TILE, TILE, ynear),
            move(l, 10, a2, p2 * big, big, core),
            move(l, 11, a2, p3 * big, TILE, core),
            move(l, 12, a2, p3 * big + TILE, TILE, core),
        ])

    def after(l, k, then):
        moves[l][k].wait_recv()
        for t in then:
            moves[l][t].start()

    def forward_first(l):
        after(l, 0, (3, 4, 5))

    def forward_rest(l):
        after(l, 3, (7, 8))
        after(l, 4, (9, 10))
        after(l, 1, (6,))
        after(l, 7, (11,))
        after(l, 9, (12,))

    def finish(l):
        for k in (2, 5, 6, 8, 10, 11, 12):
            after(l, k, ())

    def halo(slot, src, dst, hop):
        return pltpu.make_async_remote_copy(
            src_ref=src, dst_ref=dst, send_sem=halo_send.at[slot], recv_sem=halo_recv.at[slot],
            device_id=at((me + hop) % n), device_id_type=MESH_ID,
        )

    tail_copy = halo(0, xin.at[pl.ds(rows - part, part)], tail, 1)
    h1_copies = [
        halo(1 + c, u1.at[pl.ds(c * chunk, chunk)], h1.at[pl.ds(c * chunk, chunk)], hops[1])
        for c in range(chunks)
    ]
    h2_copies = [
        halo(1 + chunks + c, u2.at[pl.ds(c * chunk, chunk)], h2.at[pl.ds(c * chunk, chunk)], hops[2])
        for c in range(chunks)
    ]
    copies = [(tail_copy, 1)] + [(c, hops[1]) for c in h1_copies] + [(c, hops[2]) for c in h2_copies]

    def send_halo(copy, hop):
        @pl.when(me + hop < n)
        def _():
            copy.start()

    def take_halo(copy, hop):
        @pl.when(me >= hop)
        def _():
            copy.wait_recv()

    for l in range(layers):
        for c in loads[l]:
            c.wait()
        if l == 0:
            moves[l][0].start()
            moves[l][1].start()
            moves[l][2].start()
            x_load.wait()
            send_halo(tail_copy, hops[0])
        elif l == 1:
            moves[l][0].start()
            moves[l][1].start()
            moves[l][2].start()
        else:
            moves[l][2].start()

    @pl.when(me < hops[0])
    def _():
        tail[...] = jnp.zeros_like(tail)

    @pl.when(me < hops[1])
    def _():
        h1[...] = jnp.zeros_like(h1)

    @pl.when(me < hops[2])
    def _():
        h2[...] = jnp.zeros_like(h2)

    first = xin[...].astype(jnp.float32)
    state[...] = first
    u0[pl.ds(part, rows), :] = norm_rows(first)

    forward_first(0)
    take_halo(tail_copy, hops[0])
    u0[pl.ds(0, part), :] = norm_rows(tail[...].astype(jnp.float32))
    forward_rest(0)
    finish(0)

    def tap(l, lo):
        return w[l, :, :, lo : lo + wide].reshape(na * shard, wide)

    def now_part(l, u, lo, r0):
        pre[pl.ds(r0, chunk), :] = bias_ref[l : l + 1, :] + jnp.dot(
            u[pl.ds(lo, chunk), :], tap(l, wide), preferred_element_type=jnp.float32
        )

    def rest_part(l, earlier, r0):
        total = pre[pl.ds(r0, chunk), :] + jnp.dot(
            earlier[pl.ds(r0, chunk), :], tap(l, 0), preferred_element_type=jnp.float32
        )
        hidden = (total[:, :dim] * jax.nn.sigmoid(total[:, dim:])).astype(jnp.bfloat16)
        mix = w[l, :, :, 2 * wide :].reshape(na * shard, dim)
        return state[pl.ds(r0, chunk), :] + lax.dot_general(
            hidden, mix, (((1,), (1,)), ((), ())), preferred_element_type=jnp.float32
        )

    for c in range(chunks):
        r0 = c * chunk
        now_part(0, u0, part + r0, r0)
        new = rest_part(0, u0, r0)
        state[pl.ds(r0, chunk), :] = new
        u1[pl.ds(r0, chunk), :] = norm_rows(new)
        if c == 0:
            forward_first(1)
        send_halo(h1_copies[c], hops[1])
    moves[2][0].start()
    moves[2][1].start()
    forward_rest(1)
    finish(1)
    for c in range(chunks):
        now_part(1, u1, c * chunk, c * chunk)
    for c in range(chunks):
        r0 = c * chunk
        take_halo(h1_copies[c], hops[1])
        new = rest_part(1, h1, r0)
        state[pl.ds(r0, chunk), :] = new
        u2[pl.ds(r0, chunk), :] = norm_rows(new)
        if c == 0:
            forward_first(2)
        send_halo(h2_copies[c], hops[2])
    forward_rest(2)
    finish(2)
    for c in range(chunks):
        now_part(2, u2, c * chunk, c * chunk)
    for c in range(chunks):
        r0 = c * chunk
        take_halo(h2_copies[c], hops[2])
        out_ref[pl.ds(r0, chunk), :] = rest_part(2, h2, r0).astype(out_ref.dtype)

    for l in range(layers):
        for m in moves[l]:
            m.wait_send()
    for copy, hop in copies:
        @pl.when(me + hop < n)
        def _(copy=copy):
            copy.wait_send()


def kernel_local(na, nb, sequence_input, w_prev, w_now, conv_bias, w_mix):
    rows, dim = sequence_input.shape
    layers, shard, wide = w_prev.shape
    chunk = rows // 2
    part = DILATIONS[0]
    bf16, f32 = jnp.bfloat16, jnp.float32
    halos = 1 + 2 * (rows // chunk)
    anywhere = pl.BlockSpec(memory_space=pl.ANY)
    vmem = pl.BlockSpec(memory_space=pltpu.VMEM)
    return pl.pallas_call(
        functools.partial(block_kernel, na, nb, chunk),
        out_shape=jax.ShapeDtypeStruct((rows, dim), bf16),
        in_specs=[anywhere, anywhere, anywhere, vmem, anywhere],
        out_specs=vmem,
        scratch_shapes=[
            pltpu.VMEM((layers, na, shard, 2 * wide + dim), bf16),
            pltpu.VMEM((rows, dim), bf16),
            pltpu.VMEM((part, dim), bf16),
            pltpu.VMEM((rows, dim), f32),
            pltpu.VMEM((part + rows, dim), bf16),
            pltpu.VMEM((rows, dim), bf16),
            pltpu.VMEM((rows, dim), bf16),
            pltpu.VMEM((rows, dim), bf16),
            pltpu.VMEM((rows, dim), bf16),
            pltpu.VMEM((rows, wide), f32),
            pltpu.SemaphoreType.DMA((layers, 3)),
            pltpu.SemaphoreType.DMA,
            pltpu.SemaphoreType.DMA((layers, 13)),
            pltpu.SemaphoreType.DMA((layers, 13)),
            pltpu.SemaphoreType.DMA((halos,)),
            pltpu.SemaphoreType.DMA((halos,)),
        ],
        compiler_params=pltpu.CompilerParams(
            collective_id=0, has_side_effects=True, vmem_limit_bytes=56 * 2**20
        ),
    )(sequence_input, w_prev, w_now, conv_bias, jnp.swapaxes(w_mix, 1, 2))


def local(na, nb, sequence_input, w_prev, w_now, conv_bias, w_mix):
    rows = sequence_input.shape[0]
    shard = w_prev.shape[1]
    fits = (
        na == 4
        and nb % GROUP == 0
        and shard % TILE == 0
        and shard > GROUP * 2 * TILE
        and rows % (4 * TILE) == 0
        and DILATIONS[0] < rows
        and DILATIONS[1] % rows == 0
        and DILATIONS[2] % rows == 0
    )
    body = functools.partial(kernel_local, na, nb) if fits else plain_local
    return body(sequence_input, w_prev, w_now, conv_bias, w_mix)


def solution(mesh):
    return jax.shard_map(
        functools.partial(local, mesh.shape["seqa"], mesh.shape["seqb"]),
        mesh=mesh,
        in_specs=(
            P(("seqa", "seqb"), None),
            P(None, "seqa", None),
            P(None, "seqa", None),
            P(),
            P(None, None, "seqa"),
        ),
        out_specs=P(("seqa", "seqb"), None),
        check_vma=False,
    )
```

time: 174 us -> 85.9 us (0.49)
  Pallas kernels: 0 us -> 83 us
  waiting for transfers between devices: 77.6 us -> 0 us
  blocking collectives: 41.6 us -> 0 us
  matrix products: 20.8 us -> 0 us
  between operations: 13.7 us -> 0.01 us
  starting transfers between devices: 7.82 us -> 0 us
  local copies, waits for them, and re-layouts: 8.03 us -> 1.98 us
  other arithmetic: 2.36 us -> 0 us
    pallas_call x0 -> x1, Pallas kernels: none -> 83 us  [kernel_local(): pl.pallas_call(functools.partial(block_kernel, na, nb, chunk), out_shape=...]
    all_gather x6 -> x0, waiting for transfers between devices: 75.8 us -> none  [the longest x3 65.4 us: one_layer(): lax.all_gather(tap_prev, 'seqa', axis=0, tiled=True)]
    all_gather x3 -> x0, blocking collectives: 41.6 us -> none  [one_layer(): lax.all_gather(mixing, 'seqa', axis=1, tiled=True)]
    dot_general x9 -> x0, matrix products: 20.8 us -> none  [the longest x3 8.68 us: one_layer(): jnp.dot(earlier, lax.all_gather(tap_prev, 'seqa', axis=0, tiled=True), pr...]
    ppermute x3 -> x0, starting transfers between devices: 7.62 us -> none  [from_behind(): return lax.ppermute(value, axis, pairs)]
    slice x6 -> x0, local copies, waits for them, and re-layouts: 5.88 us -> none  [the longest x1 2.44 us: local(): w_now[layer_index]]
    convert_element_type x3 -> x0, other arithmetic: 2.14 us -> none  [norm_rows(): return (values * scale).astype(jnp.bfloat16)]
    unnamed x6 -> x0, waiting for transfers between devices: 1.79 us -> none
  transfers between devices with their start and end apart: 9 -> 0, of which waited for: 6 -> 0; matrix products, arithmetic and copies ran while one was open for 13% -> 0% of each run, Pallas kernels for 0% -> 0%
where the time goes in v1:
time: 85.9 us; the launch traced here: 84.9 us
  Pallas kernels  83 us (97%)
  local copies, waits for them, and re-layouts  1.98 us (2%)
    pallas_call x1, Pallas kernels, kernel_local(): pl.pallas_call(functools.partial(block_kernel, na, nb, chunk), out_shape=...  83 us
    unnamed x1, local copies, waits for them, and re-layouts  1.98 us

profile of v1, /device:TPU:29, one launch (start us, length us, event | category | flops | bytes accessed | tf_op | source)
XLA Modules:
  0.0 84.9 jit_solution(3566302012952518367)
XLA Ops:
  0.0 83.0 %shard_map.55 = bf16[512,640]{1,0:T(8,128)(2,1)} custom-call(bf16[512,640]{1,0:T(8,128)(2,1)} %x_hbm.1, bf16[3,160,1280]{2,1,0:T(8,128)(2,1)} %wp_hbm.1, bf16[3,160,1280]{2,1,0:T(8,128)(2,1)} %wn_hbm.1, f32[3,1280]{1,0:T(4,128)} %bias_ref.1, bf16[3,160,640]{2,1,0:T(8,128)(2,1)} %bitcast.1), custom_call_target="tpu_custom_call" | custom-call | tf_op jit(solution)/shard_map/pallas_call | solution.py:308
  83.0 2.0 %copy.7 = bf16[512,640]{1,0:T(8,128)(2,1)} copy(bf16[512,640]{1,0:T(8,128)(2,1)} %shard_map.55) | data formatting | bytes 1310720

commit v2 on v1

--- a/solution.py
+++ b/solution.py
@@ -137,19 +137,22 @@
     moves = []
     for l in range(layers):
         moves.append([
-            move(l, 0, a, p * big, big, across),
-            move(l, 1, a, direct, shard - direct, across),
-            move(l, 2, a, 0, shard, core),
-            move(l, 3, a2, p * big, big, ynear),
-            move(l, 4, a2, p * big, big, znear),
-            move(l, 5, a2, p * big, big, core),
-            move(l, 6, a2, direct, shard - direct, core),
-            move(l, 7, a2, p1 * big, TILE, znear),
-            move(l, 8, a2, p1 * big, big, core),
-            move(l, 9, a2, p2 * big + TILE, TILE, ynear),
-            move(l, 10, a2, p2 * big, big, core),
-            move(l, 11, a2, p3 * big, TILE, core),
-            move(l, 12, a2, p3 * big + TILE, TILE, core),
+            move(l, 0, a, p * big, TILE, across),
+            move(l, 1, a, p * big + TILE, TILE, across),
+            move(l, 2, a, direct, shard - direct, across),
+            move(l, 3, a, 0, shard, core),
+            move(l, 4, a2, p * big, TILE, ynear),
+            move(l, 5, a2, p * big, TILE, znear),
+            move(l, 6, a2, p * big + TILE, TILE, ynear),
+            move(l, 7, a2, p * big + TILE, TILE, znear),
+            move(l, 8, a2, p * big, big, core),
+            move(l, 9, a2, direct, shard - direct, core),
+            move(l, 10, a2, p1 * big, TILE, znear),
+            move(l, 11, a2, p1 * big, big, core),
+            move(l, 12, a2, p2 * big + TILE, TILE, ynear),
+            move(l, 13, a2, p2 * big, big, core),
+            move(l, 14, a2, p3 * big, TILE, core),
+            move(l, 15, a2, p3 * big + TILE, TILE, core),
         ])
 
     def after(l, k, then):
@@ -158,17 +161,24 @@
             moves[l][t].start()
 
     def forward_first(l):
-        after(l, 0, (3, 4, 5))
-
-    def forward_rest(l):
-        after(l, 3, (7, 8))
-        after(l, 4, (9, 10))
-        after(l, 1, (6,))
-        after(l, 7, (11,))
-        after(l, 9, (12,))
+        after(l, 0, (4, 5))
+        after(l, 1, (6, 7, 8))
+
+    def forward_second(l):
+        after(l, 4, (10,))
+        after(l, 5, ())
+        after(l, 7, (12, 13))
+        after(l, 6, (11,))
+
+    def forward_last(l):
+        after(l, 10, (14,))
+        after(l, 12, (15,))
+
+    def forward_direct(l):
+        after(l, 2, (9,))
 
     def finish(l):
-        for k in (2, 5, 6, 8, 10, 11, 12):
+        for k in (3, 8, 9, 11, 13, 14, 15):
             after(l, k, ())
 
     def halo(slot, src, dst, hop):
@@ -198,21 +208,24 @@
         def _():
             copy.wait_recv()
 
-    for l in range(layers):
-        for c in loads[l]:
-            c.wait()
-        if l == 0:
-            moves[l][0].start()
-            moves[l][1].start()
-            moves[l][2].start()
-            x_load.wait()
-            send_halo(tail_copy, hops[0])
-        elif l == 1:
-            moves[l][0].start()
-            moves[l][1].start()
-            moves[l][2].start()
-        else:
-            moves[l][2].start()
+    for c in loads[0]:
+        c.wait()
+    moves[0][0].start()
+    moves[0][1].start()
+    x_load.wait()
+    send_halo(tail_copy, hops[0])
+    for c in loads[1]:
+        c.wait()
+    moves[1][0].start()
+    moves[1][1].start()
+    moves[0][2].start()
+    moves[0][3].start()
+    for c in loads[2]:
+        c.wait()
+    moves[1][2].start()
+    moves[1][3].start()
+    for k in (0, 1, 2, 3):
+        moves[2][k].start()
 
     @pl.when(me < hops[0])
     def _():
@@ -233,7 +246,10 @@
     forward_first(0)
     take_halo(tail_copy, hops[0])
     u0[pl.ds(0, part), :] = norm_rows(tail[...].astype(jnp.float32))
-    forward_rest(0)
+    forward_second(0)
+    forward_first(1)
+    forward_last(0)
+    forward_direct(0)
     finish(0)
 
     def tap(l, lo):
@@ -257,28 +273,30 @@
     for c in range(chunks):
         r0 = c * chunk
         now_part(0, u0, part + r0, r0)
+        if c == 0:
+            forward_second(1)
         new = rest_part(0, u0, r0)
         state[pl.ds(r0, chunk), :] = new
         u1[pl.ds(r0, chunk), :] = norm_rows(new)
+        send_halo(h1_copies[c], hops[1])
         if c == 0:
-            forward_first(1)
-        send_halo(h1_copies[c], hops[1])
-    moves[2][0].start()
-    moves[2][1].start()
-    forward_rest(1)
+            forward_last(1)
+    forward_direct(1)
     finish(1)
     for c in range(chunks):
         now_part(1, u1, c * chunk, c * chunk)
+    forward_first(2)
     for c in range(chunks):
         r0 = c * chunk
         take_halo(h1_copies[c], hops[1])
         new = rest_part(1, h1, r0)
         state[pl.ds(r0, chunk), :] = new
         u2[pl.ds(r0, chunk), :] = norm_rows(new)
+        send_halo(h2_copies[c], hops[2])
         if c == 0:
-            forward_first(2)
-        send_halo(h2_copies[c], hops[2])
-    forward_rest(2)
+            forward_second(2)
+    forward_last(2)
+    forward_direct(2)
     finish(2)
     for c in range(chunks):
         now_part(2, u2, c * chunk, c * chunk)
@@ -323,8 +341,8 @@
             pltpu.VMEM((rows, wide), f32),
             pltpu.SemaphoreType.DMA((layers, 3)),
             pltpu.SemaphoreType.DMA,
-            pltpu.SemaphoreType.DMA((layers, 13)),
-            pltpu.SemaphoreType.DMA((layers, 13)),
+            pltpu.SemaphoreType.DMA((layers, 16)),
+            pltpu.SemaphoreType.DMA((layers, 16)),
             pltpu.SemaphoreType.DMA((halos,)),
             pltpu.SemaphoreType.DMA((halos,)),
         ],

time: 85.9 us -> 87 us (1.013)
  Pallas kernels: 83 us -> 84.8 us
    pallas_call x1, Pallas kernels: 83 us -> 84.8 us  [kernel_local(): pl.pallas_call(functools.partial(block_kernel, na, nb, chunk), out_shape=...]
where the time goes in v2:
time: 87 us; the launch traced here: 86.8 us
  Pallas kernels  84.8 us (97%)
  local copies, waits for them, and re-layouts  1.98 us (2%)
    pallas_call x1, Pallas kernels, kernel_local(): pl.pallas_call(functools.partial(block_kernel, na, nb, chunk), out_shape=...  84.8 us
    unnamed x1, local copies, waits for them, and re-layouts  1.98 us

profile of v2, /device:TPU:29, one launch (start us, length us, event | category | flops | bytes accessed | tf_op | source)
XLA Modules:
  0.0 86.8 jit_solution(17615824521699729462)
XLA Ops:
  0.0 84.8 %shard_map.55 = bf16[512,640]{1,0:T(8,128)(2,1)} custom-call(bf16[512,640]{1,0:T(8,128)(2,1)} %x_hbm.1, bf16[3,160,1280]{2,1,0:T(8,128)(2,1)} %wp_hbm.1, bf16[3,160,1280]{2,1,0:T(8,128)(2,1)} %wn_hbm.1, f32[3,1280]{1,0:T(4,128)} %bias_ref.1, bf16[3,160,640]{2,1,0:T(8,128)(2,1)} %bitcast.1), custom_call_target="tpu_custom_call" | custom-call | tf_op jit(solution)/shard_map/pallas_call | solution.py:326
  84.8 2.0 %copy.7 = bf16[512,640]{1,0:T(8,128)(2,1)} copy(bf16[512,640]{1,0:T(8,128)(2,1)} %shard_map.55) | data formatting | bytes 1310720

commit v3 on v2

--- a/solution.py
+++ b/solution.py
@@ -78,8 +78,8 @@
     na, nb, chunk,
     x_hbm, wp_hbm, wn_hbm, bias_ref, wm_hbm,
     out_ref,
-    w, xin, tail, state, u0, u1, u2, h1, h2, pre,
-    load_sem, x_sem, send, recv, halo_send, halo_recv,
+    w, xin, xs, state, u0, u1, u2, h1, h2, pre, osend, oin,
+    load_sem, x_sem, own_sem, send, recv, halo_send, halo_recv,
 ):
     layers, dim = wp_hbm.shape[0], x_hbm.shape[1]
     wide = 2 * dim
@@ -87,7 +87,6 @@
     rows = x_hbm.shape[0]
     n = na * nb
     part = DILATIONS[0]
-    chunks = rows // chunk
     a, b = lax.axis_index("seqa"), lax.axis_index("seqb")
     me = a * nb + b
     a1, a2 = flip(a, 1), flip(a, 2)
@@ -101,7 +100,13 @@
     def at(index):
         return (index // nb, index % nb)
 
-    hops = (1, DILATIONS[1] // rows, DILATIONS[2] // rows)
+    hop = DILATIONS[2] // rows
+    half, q = b // hop, b % hop
+    other = 1 - half
+    pair = (a, (b + hop) % nb)
+    follow_a, follow_q = (a + 1) % na, (q + 1) % hop
+    wrap = (q + 1) // hop
+    next_b = half * hop + follow_q
 
     loads = []
     for l in range(layers):
@@ -120,8 +125,12 @@
 
     barrier = pltpu.get_barrier_semaphore()
     near = [(a1, b), (a2, b), (a, b1), (a, b2)]
-    for h in sorted(set(hops)):
-        near += [at((me + h) % n), at((me + n - h) % n)]
+    near += [pair, at((me + 1) % n), at((me + n - 1) % n)]
+    near += [at((me + hop - 1) % n), at((me + n - hop + 1) % n)]
+    near += [(follow_a, b), ((a + na - 1) % na, b)]
+    near += [(a, next_b), (follow_a, next_b)]
+    last_b = half * hop + (q + hop - 1) % hop
+    near += [(a, last_b), ((a + na - 1) % na, last_b)]
     for dev in near:
         pl.semaphore_signal(barrier, inc=1, device_id=dev, device_id_type=MESH_ID)
     pl.semaphore_wait(barrier, len(near))
@@ -181,39 +190,72 @@
         for k in (3, 8, 9, 11, 13, 14, 15):
             after(l, k, ())
 
-    def halo(slot, src, dst, hop):
+    def halo(src, dst, slot, dev):
         return pltpu.make_async_remote_copy(
             src_ref=src, dst_ref=dst, send_sem=halo_send.at[slot], recv_sem=halo_recv.at[slot],
-            device_id=at((me + hop) % n), device_id_type=MESH_ID,
+            device_id=dev, device_id_type=MESH_ID,
         )
 
-    tail_copy = halo(0, xin.at[pl.ds(rows - part, part)], tail, 1)
-    h1_copies = [
-        halo(1 + c, u1.at[pl.ds(c * chunk, chunk)], h1.at[pl.ds(c * chunk, chunk)], hops[1])
-        for c in range(chunks)
-    ]
-    h2_copies = [
-        halo(1 + chunks + c, u2.at[pl.ds(c * chunk, chunk)], h2.at[pl.ds(c * chunk, chunk)], hops[2])
-        for c in range(chunks)
-    ]
-    copies = [(tail_copy, 1)] + [(c, hops[1]) for c in h1_copies] + [(c, hops[2]) for c in h2_copies]
-
-    def send_halo(copy, hop):
-        @pl.when(me + hop < n)
+    pair_low = halo(xin.at[pl.ds(part, rows - part)], xs.at[0], 0, pair)
+    pair_high = halo(xin.at[pl.ds(0, chunk)], xs.at[1, pl.ds(part, chunk)], 0, pair)
+    tail_src = xin.at[pl.ds(rows - part, part)]
+    tail_next = halo(tail_src, xs.at[0, pl.ds(0, part)], 1, at((me + 1) % n))
+    tail_back = halo(tail_src, xs.at[1, pl.ds(0, part)], 2, at((me + n - hop + 1) % n))
+    sends_next = jnp.logical_and(me + 1 < n, (b + 1) % nb < hop)
+    sends_back = jnp.logical_and(b >= hop - 1, b < 2 * hop - 1)
+    takes_next = jnp.logical_and(half == 0, me > 0)
+
+    def second(s):
+        to = s + wrap
+        slot = to % 2
+        dev = ((a + to // 2) % na, next_b)
+        return pltpu.make_async_remote_copy(
+            src_ref=u1.at[s], dst_ref=h1.at[slot], send_sem=halo_send.at[3 + slot],
+            recv_sem=halo_recv.at[3 + slot], device_id=dev, device_id_type=MESH_ID,
+        ), a + to // 2 < na
+
+    third = halo(u2.at[1], h2.at[0], 5, (follow_a, b))
+    back = halo(osend, oin, 6, pair)
+
+    def send_pair():
+        @pl.when(half == 0)
         def _():
-            copy.start()
-
-    def take_halo(copy, hop):
-        @pl.when(me >= hop)
+            pair_low.start()
+
+        @pl.when(half == 1)
         def _():
-            copy.wait_recv()
+            pair_high.start()
+
+    near_cut = (b // 2) % 2 != half
+    own_low = pltpu.make_async_copy(xin.at[pl.ds(0, chunk)], xs.at[0, pl.ds(part, chunk)], own_sem)
+    own_high = pltpu.make_async_copy(xin.at[pl.ds(part, rows - part)], xs.at[1], own_sem)
 
     for c in loads[0]:
         c.wait()
     moves[0][0].start()
     moves[0][1].start()
     x_load.wait()
-    send_halo(tail_copy, hops[0])
+
+    @pl.when(sends_next)
+    def _():
+        tail_next.start()
+
+    @pl.when(sends_back)
+    def _():
+        tail_back.start()
+
+    pl.when(near_cut)(send_pair)
+
+    @pl.when(half == 0)
+    def _():
+        own_low.start()
+        own_low.wait()
+
+    @pl.when(half == 1)
+    def _():
+        own_high.start()
+        own_high.wait()
+
     for c in loads[1]:
         c.wait()
     moves[1][0].start()
@@ -227,26 +269,32 @@
     for k in (0, 1, 2, 3):
         moves[2][k].start()
 
-    @pl.when(me < hops[0])
-    def _():
-        tail[...] = jnp.zeros_like(tail)
-
-    @pl.when(me < hops[1])
-    def _():
-        h1[...] = jnp.zeros_like(h1)
-
-    @pl.when(me < hops[2])
-    def _():
-        h2[...] = jnp.zeros_like(h2)
-
-    first = xin[...].astype(jnp.float32)
-    state[...] = first
-    u0[pl.ds(part, rows), :] = norm_rows(first)
+    @pl.when(me == 0)
+    def _():
+        xs[0, pl.ds(0, part), :] = jnp.zeros((part, dim), xs.dtype)
+
+    @pl.when(jnp.logical_and(a == 0, q == 0))
+    def _():
+        h1[0] = jnp.zeros(h1.shape[1:], h1.dtype)
+
+    @pl.when(a == 0)
+    def _():
+        h2[0] = jnp.zeros(h2.shape[1:], h2.dtype)
+
+    def enter(s):
+        block = xs[s].astype(jnp.float32)
+        u0[s] = norm_rows(block)
+        state[s] = block[part:]
 
     forward_first(0)
-    take_halo(tail_copy, hops[0])
-    u0[pl.ds(0, part), :] = norm_rows(tail[...].astype(jnp.float32))
+
+    @pl.when(takes_next)
+    def _():
+        tail_next.wait_recv()
+
+    enter(half)
     forward_second(0)
+    pl.when(jnp.logical_not(near_cut))(send_pair)
     forward_first(1)
     forward_last(0)
     forward_direct(0)
@@ -255,63 +303,96 @@
     def tap(l, lo):
         return w[l, :, :, lo : lo + wide].reshape(na * shard, wide)
 
-    def now_part(l, u, lo, r0):
-        pre[pl.ds(r0, chunk), :] = bias_ref[l : l + 1, :] + jnp.dot(
-            u[pl.ds(lo, chunk), :], tap(l, wide), preferred_element_type=jnp.float32
+    def now_part(l, now, s):
+        pre[s] = bias_ref[l : l + 1, :] + jnp.dot(
+            now, tap(l, wide), preferred_element_type=jnp.float32
         )
 
-    def rest_part(l, earlier, r0):
-        total = pre[pl.ds(r0, chunk), :] + jnp.dot(
-            earlier[pl.ds(r0, chunk), :], tap(l, 0), preferred_element_type=jnp.float32
-        )
+    def rest_part(l, earlier, s):
+        total = pre[s] + jnp.dot(earlier, tap(l, 0), preferred_element_type=jnp.float32)
         hidden = (total[:, :dim] * jax.nn.sigmoid(total[:, dim:])).astype(jnp.bfloat16)
         mix = w[l, :, :, 2 * wide :].reshape(na * shard, dim)
-        return state[pl.ds(r0, chunk), :] + lax.dot_general(
+        return state[s] + lax.dot_general(
             hidden, mix, (((1,), (1,)), ((), ())), preferred_element_type=jnp.float32
         )
 
-    for c in range(chunks):
-        r0 = c * chunk
-        now_part(0, u0, part + r0, r0)
+    for c, s in enumerate((half, other)):
+        if c == 1:
+            @pl.when(half == 1)
+            def _():
+                pair_low.wait_recv()
+
+            @pl.when(half == 0)
+            def _():
+                pair_high.wait_recv()
+                tail_back.wait_recv()
+
+            enter(s)
+        now_part(0, u0[s, pl.ds(part, chunk), :], s)
+        new = rest_part(0, u0[s, pl.ds(0, chunk), :], s)
+        state[s] = new
+        u1[s] = norm_rows(new)
+        copy, there = second(s)
+        pl.when(there)(copy.start)
         if c == 0:
             forward_second(1)
-        new = rest_part(0, u0, r0)
-        state[pl.ds(r0, chunk), :] = new
-        u1[pl.ds(r0, chunk), :] = norm_rows(new)
-        send_halo(h1_copies[c], hops[1])
-        if c == 0:
-            forward_last(1)
+    forward_last(1)
     forward_direct(1)
     finish(1)
-    for c in range(chunks):
-        now_part(1, u1, c * chunk, c * chunk)
-    forward_first(2)
-    for c in range(chunks):
-        r0 = c * chunk
-        take_halo(h1_copies[c], hops[1])
-        new = rest_part(1, h1, r0)
-        state[pl.ds(r0, chunk), :] = new
-        u2[pl.ds(r0, chunk), :] = norm_rows(new)
-        send_halo(h2_copies[c], hops[2])
+    for s in (half, other):
+        now_part(1, u1[s], s)
+    for c, s in enumerate((half, other)):
+        @pl.when(jnp.logical_or(me % nb % hop + s > 0, a > 0))
+        def _(s=s):
+            halo(u1.at[s], h1.at[s], 3 + s, pair).wait_recv()
+
+        new = rest_part(1, h1[s], s)
+        state[s] = new
+        normed = norm_rows(new)
+        u2[s] = normed
+
+        @pl.when(s == 0)
+        def _(normed=normed):
+            h2[1] = normed
+
+        @pl.when(jnp.logical_and(s == 1, a + 1 < na))
+        def _():
+            third.start()
+
         if c == 0:
-            forward_second(2)
+            forward_first(2)
+    forward_second(2)
     forward_last(2)
     forward_direct(2)
     finish(2)
-    for c in range(chunks):
-        now_part(2, u2, c * chunk, c * chunk)
-    for c in range(chunks):
-        r0 = c * chunk
-        take_halo(h2_copies[c], hops[2])
-        out_ref[pl.ds(r0, chunk), :] = rest_part(2, h2, r0).astype(out_ref.dtype)
+    for c, s in enumerate((other, half)):
+        now_part(2, u2[s], s)
+
+        @pl.when(jnp.logical_and(s == 0, a > 0))
+        def _():
+            third.wait_recv()
+
+        new = rest_part(2, h2[s], s).astype(out_ref.dtype)
+        if c == 0:
+            osend[...] = new
+            back.start()
+        else:
+            out_ref[pl.ds(pl.multiple_of(half * chunk, chunk), chunk), :] = new
+    back.wait_recv()
+    out_ref[pl.ds(pl.multiple_of(other * chunk, chunk), chunk), :] = oin[...]
 
     for l in range(layers):
         for m in moves[l]:
             m.wait_send()
-    for copy, hop in copies:
-        @pl.when(me + hop < n)
-        def _(copy=copy):
-            copy.wait_send()
+    back.wait_send()
+    for s in range(2):
+        copy, there = second(s)
+        pl.when(there)(copy.wait_send)
+    pl.when(a + 1 < na)(third.wait_send)
+    pl.when(sends_next)(tail_next.wait_send)
+    pl.when(sends_back)(tail_back.wait_send)
+    pl.when(half == 0)(pair_low.wait_send)
+    pl.when(half == 1)(pair_high.wait_send)
 
 
 def kernel_local(na, nb, sequence_input, w_prev, w_now, conv_bias, w_mix):
@@ -320,7 +401,7 @@
     chunk = rows // 2
     part = DILATIONS[0]
     bf16, f32 = jnp.bfloat16, jnp.float32
-    halos = 1 + 2 * (rows // chunk)
+    halos = 7
     anywhere = pl.BlockSpec(memory_space=pl.ANY)
     vmem = pl.BlockSpec(memory_space=pltpu.VMEM)
     return pl.pallas_call(
@@ -331,15 +412,18 @@
         scratch_shapes=[
             pltpu.VMEM((layers, na, shard, 2 * wide + dim), bf16),
             pltpu.VMEM((rows, dim), bf16),
-            pltpu.VMEM((part, dim), bf16),
-            pltpu.VMEM((rows, dim), f32),
-            pltpu.VMEM((part + rows, dim), bf16),
-            pltpu.VMEM((rows, dim), bf16),
-            pltpu.VMEM((rows, dim), bf16),
-            pltpu.VMEM((rows, dim), bf16),
-            pltpu.VMEM((rows, dim), bf16),
-            pltpu.VMEM((rows, wide), f32),
+            pltpu.VMEM((2, part + chunk, dim), bf16),
+            pltpu.VMEM((2, chunk, dim), f32),
+            pltpu.VMEM((2, part + chunk, dim), bf16),
+            pltpu.VMEM((2, chunk, dim), bf16),
+            pltpu.VMEM((2, chunk, dim), bf16),
+            pltpu.VMEM((2, chunk, dim), bf16),
+            pltpu.VMEM((2, chunk, dim), bf16),
+            pltpu.VMEM((2, chunk, wide), f32),
+            pltpu.VMEM((chunk, dim), bf16),
+            pltpu.VMEM((chunk, dim), bf16),
             pltpu.SemaphoreType.DMA((layers, 3)),
+            pltpu.SemaphoreType.DMA,
             pltpu.SemaphoreType.DMA,
             pltpu.SemaphoreType.DMA((layers, 16)),
             pltpu.SemaphoreType.DMA((layers, 16)),
@@ -361,9 +445,9 @@
         and shard % TILE == 0
         and shard > GROUP * 2 * TILE
         and rows % (4 * TILE) == 0
-        and DILATIONS[0] < rows
-        and DILATIONS[1] % rows == 0
-        and DILATIONS[2] % rows == 0
+        and rows == 4 * DILATIONS[0]
+        and DILATIONS[1] == rows
+        and 2 * DILATIONS[2] == nb * rows
     )
     body = functools.partial(kernel_local, na, nb) if fits else plain_local
     return body(sequence_input, w_prev, w_now, conv_bias, w_mix)

time: 87 us -> 86.9 us (level)
  no operation moved by 1% of the time
where the time goes in v3:
time: 86.9 us; the launch traced here: 86.7 us
  Pallas kernels  84.7 us (97%)
  local copies, waits for them, and re-layouts  1.98 us (2%)
    pallas_call x1, Pallas kernels, kernel_local(): pl.pallas_call(functools.partial(block_kernel, na, nb, chunk), out_shape=...  84.7 us
    unnamed x1, local copies, waits for them, and re-layouts  1.98 us

profile of v3, /device:TPU:29, one launch (start us, length us, event | category | flops | bytes accessed | tf_op | source)
XLA Modules:
  0.0 86.7 jit_solution(6842401066686296733)
XLA Ops:
  0.0 84.7 %shard_map.55 = bf16[512,640]{1,0:T(8,128)(2,1)} custom-call(bf16[512,640]{1,0:T(8,128)(2,1)} %x_hbm.1, bf16[3,160,1280]{2,1,0:T(8,128)(2,1)} %wp_hbm.1, bf16[3,160,1280]{2,1,0:T(8,128)(2,1)} %wn_hbm.1, f32[3,1280]{1,0:T(4,128)} %bias_ref.1, bf16[3,160,640]{2,1,0:T(8,128)(2,1)} %bitcast.1), custom_call_target="tpu_custom_call" | custom-call | tf_op jit(solution)/shard_map/pallas_call | solution.py:407
  84.7 2.0 %copy.7 = bf16[512,640]{1,0:T(8,128)(2,1)} copy(bf16[512,640]{1,0:T(8,128)(2,1)} %shard_map.55) | data formatting | bytes 1310720

commit v4 on v3

--- a/solution.py
+++ b/solution.py
@@ -119,10 +119,6 @@
         c.start()
     x_load = pltpu.make_async_copy(x_hbm, xin, x_sem)
     x_load.start()
-    for l in range(1, layers):
-        for c in loads[l]:
-            c.start()
-
     barrier = pltpu.get_barrier_semaphore()
     near = [(a1, b), (a2, b), (a, b1), (a, b2)]
     near += [pair, at((me + 1) % n), at((me + n - 1) % n)]
@@ -234,6 +230,8 @@
         c.wait()
     moves[0][0].start()
     moves[0][1].start()
+    for c in loads[1]:
+        c.start()
     x_load.wait()
 
     @pl.when(sends_next)
@@ -258,6 +256,8 @@
 
     for c in loads[1]:
         c.wait()
+    for c in loads[2]:
+        c.start()
     moves[1][0].start()
     moves[1][1].start()
     moves[0][2].start()
@@ -329,6 +329,8 @@
 
             enter(s)
         now_part(0, u0[s, pl.ds(part, chunk), :], s)
+        if c == 1:
+            forward_first(2)
         new = rest_part(0, u0[s, pl.ds(0, chunk), :], s)
         state[s] = new
         u1[s] = norm_rows(new)
@@ -341,6 +343,7 @@
     finish(1)
     for s in (half, other):
         now_part(1, u1[s], s)
+    forward_second(2)
     for c, s in enumerate((half, other)):
         @pl.when(jnp.logical_or(me % nb % hop + s > 0, a > 0))
         def _(s=s):
@@ -359,9 +362,6 @@
         def _():
             third.start()
 
-        if c == 0:
-            forward_first(2)
-    forward_second(2)
     forward_last(2)
     forward_direct(2)
     finish(2)

time: 86.9 us -> 80.1 us (0.922)
  Pallas kernels: 84.7 us -> 77.9 us
    pallas_call x1, Pallas kernels: 84.7 us -> 77.9 us  [kernel_local(): pl.pallas_call(functools.partial(block_kernel, na, nb, chunk), out_shape=...]
where the time goes in v4:
time: 80.1 us; the launch traced here: 79.9 us
  Pallas kernels  77.9 us (97%)
  local copies, waits for them, and re-layouts  1.98 us (2%)
    pallas_call x1, Pallas kernels, kernel_local(): pl.pallas_call(functools.partial(block_kernel, na, nb, chunk), out_shape=...  77.9 us
    unnamed x1, local copies, waits for them, and re-layouts  1.98 us

profile of v4, /device:TPU:29, one launch (start us, length us, event | category | flops | bytes accessed | tf_op | source)
XLA Modules:
  0.0 79.9 jit_solution(3692938481691639278)
XLA Ops:
  0.0 77.9 %shard_map.55 = bf16[512,640]{1,0:T(8,128)(2,1)} custom-call(bf16[512,640]{1,0:T(8,128)(2,1)} %x_hbm.1, bf16[3,160,1280]{2,1,0:T(8,128)(2,1)} %wp_hbm.1, bf16[3,160,1280]{2,1,0:T(8,128)(2,1)} %wn_hbm.1, f32[3,1280]{1,0:T(4,128)} %bias_ref.1, bf16[3,160,640]{2,1,0:T(8,128)(2,1)} %bitcast.1), custom_call_target="tpu_custom_call" | custom-call | tf_op jit(solution)/shard_map/pallas_call | solution.py:407
  77.9 2.0 %copy.7 = bf16[512,640]{1,0:T(8,128)(2,1)} copy(bf16[512,640]{1,0:T(8,128)(2,1)} %shard_map.55) | data formatting | bytes 1310720
